TPU v7x, 256 devices: a whole 4x4x8 slice. The times are simulated.
256 devices in a mesh: ab: 64 (over z, y, core), cd: 4 (over x).
Axes of the slice: x: 4, y: 4, z: 8, core: 2. Of those that a mesh axis runs over, the one named last changes fastest.
Arguments:
- t2_amps: float32 [1024, 8192], P('ab', 'cd'), may hold values from -6 to 6
- v_slab: float32 [65536, 8192], P('ab', 'cd'), may hold values from -0.1875 to 0.1875
- ij_irrep: int32 [1024], P('ab'), may hold values from 0 to 7, as said below
- ab_irrep: int32 [65536], P('ab'), may hold values from 0 to 7, as said below
- cd_irrep: int32 [8192], P('cd'), may hold values from 0 to 7, as said below
Outputs:
- ladder: float32 [1024, 65536], P(('ab', 'cd'))
Inputs may be any that keep to these rules, and one draw needn't show every extreme that they name: `ij_irrep`: irrep labels of D2h in any order and any counts; a pair couples only to pairs of the same label. All occupied pairs of one device may carry one label. `ab_irrep`: irrep labels of D2h in any order and any counts; all pairs of one device may carry one label. `cd_irrep`: irrep labels of D2h in any order and any counts; all pairs of one device may carry one label.
All inputs are finite; a program needn't handle non-finite values.
Results may differ from a plain program's by a relative error of at most 0.0003.
Values sent between devices are 32-bit elements; how exact they have to be, the bound alone decides.
A program may use at most 64 MiB of HBM per device.

v0:
```python
import jax
import jax.numpy as jnp
from jax import lax
from jax.sharding import PartitionSpec as P


def on_device(t2_amps, v_slab, ij_irrep, ab_irrep, cd_irrep):
    t2_sym = t2_amps * (ij_irrep[:, None] == cd_irrep[None, :]).astype(t2_amps.dtype)
    v_sym = v_slab * (ab_irrep[:, None] == cd_irrep[None, :]).astype(v_slab.dtype)
    partial_value = lax.dot_general(
        lax.all_gather(t2_sym, "ab", axis=0, tiled=True),
        v_sym,
        (((1,), (1,)), ((), ())),
        precision=lax.Precision.HIGHEST,
        preferred_element_type=jnp.float32,
    )
    n_rows = lax.axis_size("ab")
    n_cols = lax.axis_size("cd")
    width = partial_value.shape[1]
    per_dev = partial_value.shape[0] // (n_rows * n_cols)
    regrouped = partial_value.reshape(n_rows, n_cols, per_dev, width)
    regrouped = jnp.transpose(regrouped, (1, 0, 2, 3)).reshape(partial_value.shape[0], width)
    summed = lax.psum_scatter(regrouped, "cd", scatter_dimension=0, tiled=True)
    ladder = lax.all_to_all(summed, "ab", split_axis=0, concat_axis=1, tiled=True)
    return ladder


def solution(mesh):
    in_specs = (P("ab", "cd"), P("ab", "cd"), P("ab"), P("ab"), P("cd"))
    out_specs = P(("ab", "cd"), None)
    return jax.shard_map(
        on_device, mesh=mesh, in_specs=in_specs, out_specs=out_specs, check_vma=False
    )
```

profile of v0, /device:TPU:1, one launch (start us, length us, event | category | flops | bytes accessed | tf_op | source)
XLA Modules:
  0.0 240.3 jit_solution(217428079767022441)
XLA Ops:
  6.5 0.0 all-gather.2.cloned.1.call-start
  6.5 1.7 compare_select_fusion
  8.2 0.0 all-gather.2.cloned.1.call-update
  8.2 0.0 reduce-scatter.2.cloned.1.call-start
  8.3 89.1 %all-gather.2.cloned.1.call-done = f32[1024,2048]{1,0:T(8,128)} async-done(((f32[16,2048]{1,0:T(8,128)}), f32[1024,2048]{1,0:T(8,128)}) %all-gather.2.cloned.1.call-update) | async-done | bytes 8388624 | tf_op jit(solution)/shard_map/all_gather | solution.py:11
  97.3 33.1 %fusion = f32[1024,1024]{1,0:T(8,128)} fusion(f32[1024,2048]{1,0:T(8,128)} %all-gather.2.cloned.1.call-done, f32[1024,2048]{1,0:T(8,128)} %param.6, s32[2048]{0:T(1024)} %param.9, s32[1024]{0:T(1024)} %param.8), kind=kOutput, calls=%fused_computation | convolution fusion | flops 25773998080 | bytes 20983808 | tf_op jit(solution)/shard_map/dot_general | solution.py:10
  130.4 5.2 %reshape.12 = f32[64,4,4,1024]{3,2,1,0:T(4,128)} reshape(f32[1024,1024]{1,0:T(8,128)} %fusion) | data formatting | bytes 8388608 | tf_op jit(solution)/shard_map/reshape | solution.py:21
  135.6 5.5 %copy.8 = f32[64,4,4,1024]{3,2,0,1:T(4,128)} copy(f32[64,4,4,1024]{3,2,1,0:T(4,128)} %reshape.12) | data formatting | bytes 8388608 | tf_op jit(solution)/shard_map/reshape | solution.py:21
  141.0 5.3 %reshape.13 = f32[1024,1024]{1,0:T(8,128)} reshape(f32[4,64,4,1024]{3,2,1,0:T(4,128)} %bitcast.7) | data formatting | bytes 8388608 | tf_op jit(solution)/shard_map/reshape | solution.py:22
  146.3 0.0 reduce-scatter.2.cloned.1.call-update
  146.4 45.8 %reduce-scatter.2.cloned.1.call-done = f32[256,1024]{1,0:T(8,128)} async-done(((f32[1024,1024]{1,0:T(8,128)}), f32[256,1024]{1,0:T(8,128)}) %reduce-scatter.2.cloned.1.call-update) | async-done | bytes 1048592 | tf_op jit(solution)/shard_map/reduce_scatter | solution.py:23
  192.2 1.5 all_to_all.14
  193.7 38.7 %all_to_all.19 = f32[64,4,1024]{2,1,0:T(4,128)S(1)} all-to-all(f32[64,4,1024]{2,1,0:T(4,128)S(1)} %all_to_all.14), channel_id=1, replica_groups=mesh['ab'=64,'cd'=4] {'ab'}, dimensions={0} | all-to-all | bytes 2097152 | tf_op jit(solution)/shard_map/all_to_all | solution.py:24
  232.4 1.0 copy.10
Async XLA Ops:
  6.5 90.8 %all-gather.2.cloned.1.call-start = ((), (), s32[]{:S(2)}) async-start(), calls=%async_computation.2 | async-start | bytes 8519680 | tf_op jit(solution)/shard_map/all_gather | solution.py:11
  8.2 184.0 %reduce-scatter.2.cloned.1.call-start = ((), (), s32[]{:S(2)}) async-start(), calls=%async_computation.3 | async-start | bytes 5242880 | tf_op jit(solution)/shard_map/reduce_scatter | solution.py:23
Sparse Core Ops, SparseCore 0:
  10.1 87.1 all-gather.1
  146.5 45.6 reduce-scatter.1
where the time goes:
time: 241 us; the launch traced here: 240 us
  waiting for transfers between devices  135 us (56%)
  blocking collectives  38.7 us (16%)
  matrix products  33.1 us (14%)
  local copies, waits for them, and re-layouts  18.4 us (8%)
  between operations  13.4 us (6%)
    all_gather x1, waiting for transfers between devices, on_device(): lax.all_gather(t2_sym, 'ab', axis=0, tiled=True)  89.1 us
    reduce_scatter x1, waiting for transfers between devices, on_device(): summed = lax.psum_scatter(regrouped, 'cd', scatter_dimension=0, tiled=True)  45.8 us
    all_to_all x1, blocking collectives, on_device(): lax.all_to_all(summed, 'ab', split_axis=0, concat_axis=1, tiled=True)  38.7 us
    dot_general x1, matrix products, on_device(): lax.dot_general(lax.all_gather(t2_sym, 'ab', axis=0, tiled=True), v_sym,...  33.1 us
    reshape x2, local copies, waits for them, and re-layouts, on_device(): regrouped = partial_value.reshape(n_rows, n_cols, per_dev, width)  10.6 us
    reshape x1, local copies, waits for them, and re-layouts, on_device(): jnp.transpose(regrouped, (1, 0, 2, 3))  5.29 us
  transfers between devices with their start and end apart: 2, of which 2 were waited for; matrix products, arithmetic and copies ran while one was open for 0% of the time, Pallas kernels for 0%

commit v1 on v0

--- a/solution.py
+++ b/solution.py
@@ -8,7 +8,9 @@
     t2_sym = t2_amps * (ij_irrep[:, None] == cd_irrep[None, :]).astype(t2_amps.dtype)
     v_sym = v_slab * (ab_irrep[:, None] == cd_irrep[None, :]).astype(v_slab.dtype)
     partial_value = lax.dot_general(
-        lax.all_gather(t2_sym, "ab", axis=0, tiled=True),
+        jnp.concatenate(
+            lax.all_to_all(jnp.stack([t2_sym] * lax.axis_size("ab")), "ab", 0, 0), axis=0
+        ),
         v_sym,
         (((1,), (1,)), ((), ())),
         precision=lax.Precision.HIGHEST,

time: 241 us -> 359 us (1.49)
  blocking collectives: 38.7 us -> 236 us
  waiting for transfers between devices: 135 us -> 47.1 us
  matrix products: 33.1 us -> 42.7 us
    all_to_all x0 -> x1, blocking collectives: none -> 197 us  [on_device(): lax.all_to_all(jnp.stack([t2_sym] * lax.axis_size('ab')), 'ab', 0, 0)]
    all_gather x1 -> x0, waiting for transfers between devices: 89.1 us -> none  [on_device(): lax.all_gather(t2_sym, 'ab', axis=0, tiled=True)]
    reshape x2 -> x0, local copies, waits for them, and re-layouts: 10.6 us -> none  [on_device(): regrouped = partial_value.reshape(n_rows, n_cols, per_dev, width)]
    dot_general x1, matrix products: 33.1 us -> 42.7 us  [on_device(): lax.dot_general(jnp.concatenate(lax.all_to_all(jnp.stack([t2_sym] * lax.a...]
    all_to_all x0 -> x1, local copies, waits for them, and re-layouts: none -> 4.86 us  [on_device(): lax.all_to_all(jnp.stack([t2_sym] * lax.axis_size('ab')), 'ab', 0, 0)]
    transpose x0 -> x1, local copies, waits for them, and re-layouts: none -> 4.67 us  [on_device(): jnp.transpose(regrouped, (1, 0, 2, 3))]
  transfers between devices with their start and end apart: 2 -> 1, of which waited for: 2 -> 1; matrix products, arithmetic and copies ran while one was open for 0% -> 0% of each run, Pallas kernels for 0% -> 0%
where the time goes in v1:
time: 359 us
  blocking collectives  236 us (66%)
  waiting for transfers between devices  47.1 us (13%)
  matrix products  42.7 us (12%)
  local copies, waits for them, and re-layouts  18.3 us (5%)
  between operations  13.4 us (4%)
    all_to_all x1, blocking collectives, on_device(): lax.all_to_all(jnp.stack([t2_sym] * lax.axis_size('ab')), 'ab', 0, 0)  197 us
    reduce_scatter x1, waiting for transfers between devices, on_device(): summed = lax.psum_scatter(regrouped, 'cd', scatter_dimension=0, tiled=True)  47.1 us
    dot_general x1, matrix products, on_device(): lax.dot_general(jnp.concatenate(lax.all_to_all(jnp.stack([t2_sym] * lax.a...  42.7 us
    all_to_all x1, blocking collectives, on_device(): lax.all_to_all(summed, 'ab', split_axis=0, concat_axis=1, tiled=True)  38.7 us
  transfers between devices with their start and end apart: 1, of which 1 were waited for; matrix products, arithmetic and copies ran while one was open for 0% of the time, Pallas kernels for 0%

profile of v1, /device:TPU:1, one launch (start us, length us, event | category | flops | bytes accessed | tf_op | source)
XLA Modules:
  0.0 358.7 jit_solution(4811865304627761373)
XLA Ops:
  6.5 0.0 reduce-scatter.2.cloned.1.call-start
  6.5 1.0 compare_select_fusion
  7.5 1.0 stack.2
  8.6 197.5 %all_to_all.24 = f32[64,16,2048]{2,1,0:T(8,128)S(1)} all-to-all(f32[64,16,2048]{2,1,0:T(8,128)S(1)} %stack.2), channel_id=1, replica_groups=mesh['ab'=64,'cd'=4] {'ab'}, dimensions={0} | all-to-all | bytes 16777216 | tf_op jit(solution)/shard_map/all_to_all | solution.py:12
  206.1 0.0 copy-start
  206.1 0.0 copy-start.1
  206.1 4.9 %copy.7 = f32[64,16,2048]{2,0,1:T(8,128)S(1)} copy(f32[64,16,2048]{2,1,0:T(8,128)S(1)} %all_to_all.24) | data formatting | bytes 16777216 | tf_op jit(solution)/shard_map/all_to_all | solution.py:12
  210.9 0.0 copy-done
  210.9 0.0 copy-done.1
  210.9 42.7 %fusion.7 = f32[4,64,4,1024]{3,1,2,0:T(8,128)S(1)} fusion(f32[64,4,4,2048]{3,0,2,1:T(8,128)S(1)} %bitcast.14, f32[1024,2048]{1,0:T(8,128)} %param.6, s32[2048]{0:T(1024)S(1)} %copy-done, s32[1024]{0:T(1024)S(1)} %copy-done.1), kind=kOutput, calls=%fused_computation.7 | convolution fusion | flops 25773998080 | bytes 20983808 | tf_op jit(solution)/shard_map/dot_general | solution.py:10
  253.6 4.7 %copy.8 = f32[4,64,4,1024]{3,2,1,0:T(4,128)} copy(f32[4,64,4,1024]{3,1,2,0:T(8,128)S(1)} %fusion.7) | data formatting | bytes 8388608 | tf_op jit(solution)/shard_map/transpose | solution.py:24
  258.3 5.3 %reshape.15 = f32[1024,1024]{1,0:T(8,128)} reshape(f32[4,64,4,1024]{3,2,1,0:T(4,128)} %copy.8) | data formatting | bytes 8388608 | tf_op jit(solution)/shard_map/reshape | solution.py:24
  263.6 0.0 reduce-scatter.2.cloned.1.call-update
  263.6 47.1 %reduce-scatter.2.cloned.1.call-done = f32[256,1024]{1,0:T(8,128)} async-done(((f32[1024,1024]{1,0:T(8,128)}), f32[256,1024]{1,0:T(8,128)}) %reduce-scatter.2.cloned.1.call-update) | async-done | bytes 1048592 | tf_op jit(solution)/shard_map/reduce_scatter | solution.py:25
  310.7 1.5 all_to_all.18
  312.2 38.7 %all_to_all.25 = f32[64,4,1024]{2,1,0:T(4,128)S(1)} all-to-all(f32[64,4,1024]{2,1,0:T(4,128)S(1)} %all_to_all.18), channel_id=1, replica_groups=mesh['ab'=64,'cd'=4] {'ab'}, dimensions={0} | all-to-all | bytes 2097152 | tf_op jit(solution)/shard_map/all_to_all | solution.py:26
  350.9 1.0 copy.11
Async XLA Ops:
  6.5 304.1 %reduce-scatter.2.cloned.1.call-start = ((), (), s32[]{:S(2)}) async-start(), calls=%async_computation.3 | async-start | bytes 5242880 | tf_op jit(solution)/shard_map/reduce_scatter | solution.py:25
  206.1 4.9 %copy-start = (s32[2048]{0:T(1024)S(1)}, s32[2048]{0:T(1024)}, u32[]{:S(2)}) copy-start(s32[2048]{0:T(1024)} %param.9) | copy-start | bytes 24580
  206.1 4.9 %copy-start.1 = (s32[1024]{0:T(1024)S(1)}, s32[1024]{0:T(1024)}, u32[]{:S(2)}) copy-start(s32[1024]{0:T(1024)} %param.8) | copy-start | bytes 12292
Sparse Core Ops, SparseCore 0:
  263.7 46.9 reduce-scatter.1
